TPU v7x, 128 devices: a whole 4x4x4 slice. The times are simulated.
128 devices in a mesh: req: 4 (over y), tm: 32 (over z, x, core).
Axes of the slice: x: 4, y: 4, z: 4, core: 2. Of those that a mesh axis runs over, the one named last changes fastest.
Arguments:
- latents: bfloat16 [128, 12288], P('req', 'tm'), may hold values from -6 to 6
- lengths: int32 [8], replicated, may hold values from 1 to 21, 128 in all
- w_in: bfloat16 [3, 3, 3, 16, 384], replicated, may hold values from -0.3125 to 0.3125
- b_in: float32 [384], replicated, may hold values from -3 to 3
- w_mid: bfloat16 [3, 3, 3, 384, 384], replicated, may hold values from -0.0625 to 0.0625
- b_mid: float32 [384], replicated, may hold values from -3 to 3
Outputs:
- decoded: bfloat16 [128, 64, 48, 384], P(('req', 'tm'))
Inputs may be any that keep to these rules, and one draw needn't show every extreme that they name: Request lengths in latent frames, in order along the frames, summing to 128; the longest has exactly 21.
All inputs are finite; a program needn't handle non-finite values.
Results may differ from a plain program's by a relative error of at most 0.0041.
Values may be sent and summed in bfloat16 or wider, within the bound.
No kernel may reach another device: no remote copies, remote signals or barrier semaphores. Data moves between devices by JAX's collectives and lax.ppermute only.
A program may use at most 192 MiB of HBM per device.

v0:
```python
import jax
import jax.numpy as jnp
from jax import lax
from jax.experimental import pallas as pl
from jax.experimental.pallas import tpu as pltpu
from jax.sharding import PartitionSpec as P

C = 16
HT = 32
WT = 24
CH = 384
BF = jnp.bfloat16
F32 = jnp.float32
KIN = 27 * C
KMID = 3 * CH
SUMS = (1, 2, 2)
STRIP = 4
SW = WT // STRIP
VMEM_LIMIT = 44 * 2**20
PITCH = WT + 1
TOP = 32
MROW = 832


def prep_body(w_ref, ss_ref, ds_ref, sd_ref):
    w = [[w_ref[0, p, q].astype(F32) for q in range(3)] for p in range(3)]
    by_row = []
    for p in range(3):
        by_row.append((w[p][0] + w[p][1] + w[p][2], w[p][0], w[p][2]))
    rows = lambda k: by_row[0][k] + by_row[1][k] + by_row[2][k]
    ss_ref[...] = rows(0).astype(BF)
    ds_ref[:, 0:CH] = rows(1).astype(BF)
    ds_ref[:, CH : 2 * CH] = rows(2).astype(BF)
    sd_ref[:, 0:CH] = by_row[0][0].astype(BF)
    sd_ref[:, CH : 2 * CH] = by_row[2][0].astype(BF)


def prep(w_mid):
    rows = 128
    per = CH // rows
    return pl.pallas_call(
        prep_body,
        grid=(3 * per,),
        in_specs=[
            pl.BlockSpec((1, 3, 3, rows, CH), lambda n: (n // per, 0, 0, n % per, 0))
        ],
        out_specs=[pl.BlockSpec((rows, k * CH), lambda n: (n, 0)) for k in SUMS],
        out_shape=[pltpu.HBM((KMID, k * CH), BF) for k in SUMS],
        compiler_params=pltpu.CompilerParams(vmem_limit_bytes=16 * 2**20),
        name="prep",
    )(w_mid)


def slots_body(before_ref, own_ref, o_ref, rows, out):
    for c in range(3):
        lanes = slice(c * 128, (c + 1) * 128)
        rows[c, 0:8, :] = before_ref[:, lanes].astype(F32)[HT - 8 : HT]
        rows[c, 8 : 8 + HT, :] = own_ref[:, lanes].astype(F32)
        for k in range(8):
            piece = rows[c, 4 + k : 4 + k + HT, :] if k < 5 else jnp.zeros((HT, 128), F32)
            out[c, pl.ds(k, HT, stride=8), :] = piece
        o_ref[:, :, lanes] = out[c].reshape(HT, 8, 128).astype(BF)


def slots(before, own):
    return pl.pallas_call(
        slots_body,
        out_shape=jax.ShapeDtypeStruct((HT, 8, CH), BF),
        scratch_shapes=[pltpu.VMEM((3, HT + 8, 128), F32), pltpu.VMEM((3, HT * 8, 128), F32)],
        compiler_params=pltpu.CompilerParams(vmem_limit_bytes=8 * 2**20),
        name="slots",
    )(before, own)


def main_body(
    pos_ref, len_ref, x_ref, win_ref, bin_ref, bmid_ref, ss_hbm, ds_hbm, sd_hbm, w_hbm, out_hbm,
    xf, xp, zt, at, hf, hb, dc, dr, dd, w_ss, w_ds, w_sd, w_dd, r_ss, r_ds, r_sd, r_dd, st, ob, wsem, osem,
):
    sums = [
        pltpu.make_async_copy(src, dst, wsem.at[k])
        for k, (src, dst) in enumerate(((ss_hbm, w_ss), (ds_hbm, w_ds), (sd_hbm, w_sd)))
    ]
    outer = [
        pltpu.make_async_copy(w_hbm.at[t, p, q], w_dd.at[k, pl.ds(t * CH, CH)], wsem.at[3 + 3 * k + t])
        for k, (p, q) in enumerate(((0, 0), (0, 2), (2, 0), (2, 2)))
        for t in range(3)
    ]
    for cp in sums + outer:
        cp.start()

    first = pos_ref[0] - 4
    rid = [jnp.int32(0)] * 5
    end = jnp.int32(0)
    for r in range(8):
        end = end + len_ref[r]
        rid = [rid[k] + (first + k >= end).astype(jnp.int32) for k in range(5)]
    ok = lambda k, g: ((first + k >= 0) & (rid[k] == rid[g])).astype(F32)
    m_in = [[ok(g + t, g + 2) if t < 2 else None for t in range(3)] for g in range(3)]
    m_mid = [ok(2, 4), ok(3, 4), None]
    bias = lambda ref, c: ref[pl.ds(c * 128, 128)].reshape(1, 128)
    times = lambda v, m: v if m is None else v * m

    for c in range(3):
        xf[c] = x_ref[:, :, c * 128 : (c + 1) * 128].reshape(HT * 8, 128).astype(F32)
    for f in range(5):
        x = [xf[c, pl.ds(f, HT, stride=8), :] for c in range(3)]
        x = jnp.concatenate([jnp.zeros((HT, C), F32)] + x + [jnp.zeros((HT, 128 - C), F32)], axis=1)
        for s in range(STRIP):
            k = f * STRIP + s
            xp[k, 0:8, :] = jnp.zeros((8, 128), F32)
            xp[k, 8 : 8 + HT, :] = x[:, s * SW * C : s * SW * C + 128]
            xp[k, 8 + HT : 16 + HT, :] = jnp.zeros((8, 128), F32)

    for t in range(3):
        for p in range(3):
            for b in range(3):
                block = []
                for k in range(4 * b, 4 * b + 4):
                    s, g = k // 3, k % 3
                    block.append(times(xp[(g + t) * STRIP + s, 7 + p : 7 + p + HT, :], m_in[g][t]))
                z = jnp.concatenate(block, axis=0)
                zt[3 * t + p, :, b * 128 : (b + 1) * 128] = z.T.astype(BF)

    for tp in range(9):
        for j in range(SW):
            at[tp * 48 : (tp + 1) * 48, j * CH : (j + 1) * CH] = zt[tp, 16 * j : 16 * j + 48, :]

    for k in range(9):
        hf[k, 0:TOP, :] = jnp.zeros((TOP, 128), F32)
        hf[k, pl.ds(TOP + WT, HT, stride=PITCH), :] = jnp.zeros((HT, 128), F32)
        hf[k, TOP + HT * PITCH : TOP + MROW, :] = jnp.zeros((MROW - HT * PITCH, 128), F32)

    for n in range(SW // 2):
        a = at[:, n * 2 * CH : (n + 1) * 2 * CH]
        v = lax.dot_general(a, win_ref[...], (((0,), (0,)), ((), ())), preferred_element_type=F32)
        for k in range(2 * STRIP * 3):
            s, g, j = k // 3 % STRIP, k % 3, n * 2 + k // (3 * STRIP)
            for c in range(3):
                u = v[k * HT : (k + 1) * HT, c * 128 : (c + 1) * 128]
                u = 0.5 * (u + bias(bin_ref, c))
                u = times(u * (1.0 + jnp.tanh(u)), m_mid[g]).astype(BF).astype(F32)
                hf[3 * g + c, pl.ds(TOP + s * SW + j, HT, stride=PITCH), :] = u

    for cp in sums + outer:
        cp.wait()

    half = MROW // 2
    for k in range(9):
        lanes = slice(k * 128, (k + 1) * 128)
        for lo in range(0, MROW, half):
            rows = slice(lo, lo + half)
            h = lambda back: hf[k, TOP + lo - back : TOP + lo + half - back, :]
            col = h(0) - h(1)
            hb[rows, lanes] = h(0).astype(BF)
            dc[rows, lanes] = col.astype(BF)
            dr[rows, lanes] = (h(0) - h(PITCH)).astype(BF)
            dd[rows, lanes] = (col - (h(PITCH) - h(PITCH + 1))).astype(BF)

    def mm(out, lhs, rows, w):
        v = jnp.dot(lhs[0:rows, :], w, preferred_element_type=F32)
        for k in range(v.shape[1] // 128):
            part = v[:, k * 128 : (k + 1) * 128]
            out[k] = part + bias(bmid_ref, k) if out is r_ss else part

    mm(r_ss, hb, HT * PITCH, w_ss[...])
    mm(r_ds, dc, HT * PITCH, w_ds[...])
    mm(r_sd, dr, MROW, w_sd[...])

    mm(r_dd, dd, MROW, jnp.concatenate([w_dd[k] for k in range(4)], axis=1))

    def emit(i, c):
        at_row = lambda ref, k, off: ref[k, i * PITCH + off : i * PITCH + off + WT, :]
        slot = i % 4
        ss = at_row(r_ss, c, 0)
        t0 = ss - at_row(r_ds, c, 0)
        t1 = ss + at_row(r_ds, 3 + c, 1)
        above = at_row(r_sd, c, 0)
        under = at_row(r_sd, 3 + c, PITCH)
        st[c, slot, 0, pl.ds(0, WT, stride=2), :] = t0 - (above - at_row(r_dd, c, 0))
        st[c, slot, 0, pl.ds(1, WT, stride=2), :] = t1 - (above + at_row(r_dd, 3 + c, 1))
        st[c, slot, 1, pl.ds(0, WT, stride=2), :] = t0 + (under - at_row(r_dd, 6 + c, PITCH))
        st[c, slot, 1, pl.ds(1, WT, stride=2), :] = t1 + (under + at_row(r_dd, 9 + c, PITCH + 1))
        for a in range(2):
            ob[2 * i + a, :, c * 128 : (c + 1) * 128] = st[c, slot, a].astype(BF)

    for i in range(HT):
        for c in range(3):
            emit(i, c)
        if i % 8 == 7:
            block = pl.ds(2 * (i - 7), 16)
            pltpu.make_async_copy(ob.at[block], out_hbm.at[0, block], osem).start()
    pltpu.make_async_copy(ob, out_hbm.at[0], osem).wait()


def decode(pos, lengths, x, w_in, b_in, b_mid, ss, ds, sd, w_mid):
    smem = pl.BlockSpec(memory_space=pltpu.SMEM)
    vmem = pl.BlockSpec(memory_space=pltpu.VMEM)
    hbm = pl.BlockSpec(memory_space=pl.ANY)
    return pl.pallas_call(
        main_body,
        in_specs=[smem, smem, vmem, vmem, vmem, vmem, hbm, hbm, hbm, hbm],
        out_specs=hbm,
        out_shape=jax.ShapeDtypeStruct((1, 2 * HT, 2 * WT, CH), BF),
        scratch_shapes=[
            pltpu.VMEM((3, HT * 8, 128), F32),
            pltpu.VMEM((5 * STRIP, HT + 16, 128), F32),
            pltpu.VMEM((9, 128, CH), BF),
            pltpu.VMEM((KIN, SW * CH), BF),
            pltpu.VMEM((9, TOP + MROW, 128), F32),
            pltpu.VMEM((MROW, KMID), BF),
            pltpu.VMEM((MROW, KMID), BF),
            pltpu.VMEM((MROW, KMID), BF),
            pltpu.VMEM((MROW, KMID), BF),
            pltpu.VMEM((KMID, CH), BF),
            pltpu.VMEM((KMID, 2 * CH), BF),
            pltpu.VMEM((KMID, 2 * CH), BF),
            pltpu.VMEM((4, KMID, CH), BF),
            pltpu.VMEM((3, HT * PITCH, 128), F32),
            pltpu.VMEM((6, HT * PITCH, 128), F32),
            pltpu.VMEM((6, MROW, 128), F32),
            pltpu.VMEM((12, MROW, 128), F32),
            pltpu.VMEM((3, 4, 2, 2 * WT, 128), F32),
            pltpu.VMEM((2 * HT, 2 * WT, CH), BF),
            pltpu.SemaphoreType.DMA((15,)),
            pltpu.SemaphoreType.DMA,
        ],
        compiler_params=pltpu.CompilerParams(vmem_limit_bytes=VMEM_LIMIT),
        name="decode",
    )(pos, lengths, x, w_in, b_in, b_mid, ss, ds, sd, w_mid)


def on_device(latents, lengths, w_in, b_in, w_mid, b_mid):
    groups = lax.axis_size("req")
    before = lax.ppermute(latents, "req", [(i, i + 1) for i in range(groups - 1)])
    x = lax.all_to_all(slots(before, latents), "tm", split_axis=0, concat_axis=0, tiled=True)
    w_mid = pltpu.with_memory_space_constraint(w_mid, pltpu.HBM)
    sums = [pltpu.with_memory_space_constraint(w, pltpu.HBM) for w in prep(w_mid)]
    pos = lax.axis_index(("req", "tm")).astype(jnp.int32).reshape(1)
    return decode(pos, lengths, x, w_in.reshape(KIN, CH), b_in, b_mid, *sums, w_mid)


def solution(mesh):
    in_specs = (P("req", "tm"), P(), P(), P(), P(), P())
    out_specs = P(("req", "tm"), None, None, None)
    return jax.shard_map(
        on_device, mesh=mesh, in_specs=in_specs, out_specs=out_specs, check_vma=False
    )
```

profile of v0, /device:TPU:1, one launch (start us, length us, event | category | flops | bytes accessed | tf_op | source)
XLA Modules:
  0.0 39.8 jit_solution(7450531030586530036)
XLA Ops:
  0.0 4.0 %collective-permute-start = (bf16[32,384]{1,0:T(8,128)(2,1)}, bf16[32,384]{1,0:T(8,128)(2,1)S(1)}, u32[]{:S(2)}, u32[]{:S(2)}) collective-permute-start(bf16[32,384]{1,0:T(8,128)(2,1)} %own_ref.1), channel_id=1, source_target_pairs={{0,32},{32,64},{64,96},{1,33},{33,65},{65,97},{2,34},{34,66},{66,9... | collective-permute-start | bytes 73736 | tf_op jit(solution)/shard_map/ppermute | solution.py:234
  4.0 1.1 %collective-permute-done.before_ref = bf16[32,384]{1,0:T(8,128)(2,1)S(1)} collective-permute-done((bf16[32,384]{1,0:T(8,128)(2,1)}, bf16[32,384]{1,0:T(8,128)(2,1)S(1)}, u32[]{:S(2)}, u32[]{:S(2)}) %collective-permute-start) | collective-permute-done | bytes 24608 | tf_op jit(solution)/shard_map/ppermute | solution.py:234
  5.2 0.0 copy-start.1
  5.2 0.7 %copy-done.1 = bf16[32,384]{1,0:T(8,128)(2,1)S(1)} copy-done((bf16[32,384]{1,0:T(8,128)(2,1)S(1)}, bf16[32,384]{1,0:T(8,128)(2,1)}, u32[]{:S(2)}) %copy-start.1) | copy-done | bytes 24600
  5.9 0.8 %slots.1 = bf16[32,8,384]{2,1,0:T(8,128)(2,1)} custom-call(bf16[32,384]{1,0:T(8,128)(2,1)S(1)} %collective-permute-done.before_ref, bf16[32,384]{1,0:T(8,128)(2,1)S(1)} %copy-done.1), custom_call_target="tpu_custom_call" | custom-call | tf_op jit(solution)/shard_map/slots/pallas_call | solution.py:66
  6.7 9.5 %all-to-all-start = ((bf16[32,8,384]{2,1,0:T(8,128)(2,1)}), bf16[32,8,384]{2,1,0:T(8,128)(2,1)S(1)}, u32[]{:S(2)}, u32[]{:S(2)}) async-start(bf16[32,8,384]{2,1,0:T(8,128)(2,1)} %slots.1), calls=%async_computation | async-start | bytes 393216 | tf_op jit(solution)/shard_map/all_to_all | solution.py:235
  16.1 0.0 copy-start
  16.2 0.0 copy-start.2
  16.2 0.0 copy-start.3
  16.2 0.0 copy-start.4
  16.2 8.6 %prep.1 = (bf16[1152,384]{1,0:T(8,128)(2,1)}, bf16[1152,768]{1,0:T(8,128)(2,1)}, bf16[1152,768]{1,0:T(8,128)(2,1)}) custom-call(bf16[3,3,3,384,384]{4,3,2,1,0:T(8,128)(2,1)} %w_hbm.1), custom_call_target="tpu_custom_call" | custom-call | tf_op jit(solution)/shard_map/prep/pallas_call | solution.py:41
  24.8 0.0 all-to-all-done.x_ref
  24.8 0.0 copy-done
  24.8 0.0 copy-done.2
  24.8 0.0 copy-done.3
  24.8 0.0 copy-done.4
  24.8 15.0 %decode.1 = bf16[1,64,48,384]{3,2,1,0:T(8,128)(2,1)} custom-call(s32[1]{0:T(128)} %bitcast.pos_ref, s32[8]{0:T(128)S(1)} %copy-done.4, bf16[32,8,384]{2,1,0:T(8,128)(2,1)S(1)} %all-to-all-done.x_ref, bf16[432,384]{1,0:T(8,128)(2,1)S(1)} %bitcast.2, f32[384]{0:T(512)S(1)} %copy-done.2, f32[384]{0:T(512)S(1)} %copy-done.3, ...), custom_call_target="tpu_custom_call" | custom-call | tf_op jit(solution)/shard_map/decode/pallas_call | solution.py:199
Async XLA Ops:
  0.0 5.2 %collective-permute-start = (bf16[32,384]{1,0:T(8,128)(2,1)}, bf16[32,384]{1,0:T(8,128)(2,1)S(1)}, u32[]{:S(2)}, u32[]{:S(2)}) collective-permute-start(bf16[32,384]{1,0:T(8,128)(2,1)} %own_ref.1), channel_id=1, source_target_pairs={{0,32},{32,64},{64,96},{1,33},{33,65},{65,97},{2,34},{34,66},{66,9... | collective-permute-start | bytes 73736 | tf_op jit(solution)/shard_map/ppermute | solution.py:234
  5.2 0.7 %copy-start.1 = (bf16[32,384]{1,0:T(8,128)(2,1)S(1)}, bf16[32,384]{1,0:T(8,128)(2,1)}, u32[]{:S(2)}) copy-start(bf16[32,384]{1,0:T(8,128)(2,1)} %own_ref.1) | copy-start | bytes 73732
  6.7 18.1 %all-to-all-start = ((bf16[32,8,384]{2,1,0:T(8,128)(2,1)}), bf16[32,8,384]{2,1,0:T(8,128)(2,1)S(1)}, u32[]{:S(2)}, u32[]{:S(2)}) async-start(bf16[32,8,384]{2,1,0:T(8,128)(2,1)} %slots.1), calls=%async_computation | async-start | bytes 393216 | tf_op jit(solution)/shard_map/all_to_all | solution.py:235
  16.1 8.6 %copy-start = (bf16[3,3,3,16,384]{4,3,2,1,0:T(8,128)(2,1)S(1)}, bf16[3,3,3,16,384]{4,3,2,1,0:T(8,128)(2,1)}, u32[]{:S(2)}) copy-start(bf16[3,3,3,16,384]{4,3,2,1,0:T(8,128)(2,1)} %param.8) | copy-start | bytes 995332
  16.2 8.6 %copy-start.2 = (f32[384]{0:T(512)S(1)}, f32[384]{0:T(512)}, u32[]{:S(2)}) copy-start(f32[384]{0:T(512)} %bin_ref.1) | copy-start | bytes 4612
  16.2 8.6 %copy-start.3 = (f32[384]{0:T(512)S(1)}, f32[384]{0:T(512)}, u32[]{:S(2)}) copy-start(f32[384]{0:T(512)} %bmid_ref.1) | copy-start | bytes 4612
  16.2 8.6 %copy-start.4 = (s32[8]{0:T(128)S(1)}, s32[8]{0:T(128)}, u32[]{:S(2)}) copy-start(s32[8]{0:T(128)} %len_ref.1) | copy-start | bytes 100
where the time goes:
time: 40.3 us; the launch traced here: 39.8 us
  Pallas kernels  24.4 us (61%)
  starting transfers between devices  13.5 us (33%)
  waiting for transfers between devices  1.14 us (3%)
  local copies, waits for them, and re-layouts  0.76 us (2%)
    pallas_call x1, Pallas kernels, decode(): pl.pallas_call(main_body, in_specs=[smem, smem, vmem, vmem, vmem, vmem, h...  15 us
    all_to_all x1, starting transfers between devices, on_device(): lax.all_to_all(slots(before, latents), 'tm', split_axis=0, concat_axis=0,...  9.45 us
    pallas_call x1, Pallas kernels, prep(): pl.pallas_call(prep_body, grid=(3 * per,), in_specs=[pl.BlockSpec((1, 3,...  8.57 us
    ppermute x1, starting transfers between devices, on_device(): lax.ppermute(latents, 'req', [(i, i + 1) for i in range(groups - 1)])  4.01 us
    ppermute x1, waiting for transfers between devices, on_device(): lax.ppermute(latents, 'req', [(i, i + 1) for i in range(groups - 1)])  1.14 us
  transfers between devices with their start and end apart: 2, of which 1 were waited for; matrix products, arithmetic and copies ran while one was open for 0% of the time, Pallas kernels for 22%

commit v1 on v0

--- a/solution.py
+++ b/solution.py
@@ -13,7 +13,6 @@
 F32 = jnp.float32
 KIN = 27 * C
 KMID = 3 * CH
-SUMS = (1, 2, 2)
 STRIP = 4
 SW = WT // STRIP
 VMEM_LIMIT = 44 * 2**20
@@ -22,39 +21,59 @@
 MROW = 832
 
 
-def prep_body(w_ref, ss_ref, ds_ref, sd_ref):
-    w = [[w_ref[0, p, q].astype(F32) for q in range(3)] for p in range(3)]
-    by_row = []
-    for p in range(3):
-        by_row.append((w[p][0] + w[p][1] + w[p][2], w[p][0], w[p][2]))
-    rows = lambda k: by_row[0][k] + by_row[1][k] + by_row[2][k]
-    ss_ref[...] = rows(0).astype(BF)
-    ds_ref[:, 0:CH] = rows(1).astype(BF)
-    ds_ref[:, CH : 2 * CH] = rows(2).astype(BF)
-    sd_ref[:, 0:CH] = by_row[0][0].astype(BF)
-    sd_ref[:, CH : 2 * CH] = by_row[2][0].astype(BF)
+def prep_body(w_hbm, ss_ref, ds_ref, sd_hbm, w, sd, isem, osem):
+    rows = 128
+    parts = [(t, slice(r, r + rows)) for t in range(3) for r in range(0, CH, rows)]
+    reads, writes = [], []
+    for n, (t, r) in enumerate(parts):
+        cp = pltpu.make_async_copy(w_hbm.at[t, :, :, r], w.at[t, :, :, r], isem.at[n])
+        cp.start()
+        reads.append(cp)
+    for n, (t, r) in enumerate(parts):
+        reads[n].wait()
+        out = slice(n * rows, (n + 1) * rows)
+        tap = lambda p, q: w[t, p, q, r].astype(F32)
+        col = [[tap(p, q) for p in range(3)] for q in range(3)]
+        col_sum = [c[0] + c[1] + c[2] for c in col]
+        ss_ref[out] = (col_sum[0] + col_sum[1] + col_sum[2]).astype(BF)
+        ds_ref[out, 0:CH] = col_sum[0].astype(BF)
+        ds_ref[out, CH : 2 * CH] = col_sum[2].astype(BF)
+        sd[out, 0:CH] = (col[0][0] + col[1][0] + col[2][0]).astype(BF)
+        sd[out, CH : 2 * CH] = (col[0][2] + col[1][2] + col[2][2]).astype(BF)
+        cp = pltpu.make_async_copy(sd.at[out], sd_hbm.at[out], osem.at[n])
+        cp.start()
+        writes.append(cp)
+    for cp in writes:
+        cp.wait()
 
 
 def prep(w_mid):
-    rows = 128
-    per = CH // rows
+    vmem = pl.BlockSpec(memory_space=pltpu.VMEM)
+    hbm = pl.BlockSpec(memory_space=pl.ANY)
     return pl.pallas_call(
         prep_body,
-        grid=(3 * per,),
-        in_specs=[
-            pl.BlockSpec((1, 3, 3, rows, CH), lambda n: (n // per, 0, 0, n % per, 0))
+        in_specs=[hbm],
+        out_specs=[vmem, vmem, hbm],
+        out_shape=[
+            jax.ShapeDtypeStruct((KMID, CH), BF),
+            jax.ShapeDtypeStruct((KMID, 2 * CH), BF),
+            pltpu.HBM((KMID, 2 * CH), BF),
         ],
-        out_specs=[pl.BlockSpec((rows, k * CH), lambda n: (n, 0)) for k in SUMS],
-        out_shape=[pltpu.HBM((KMID, k * CH), BF) for k in SUMS],
-        compiler_params=pltpu.CompilerParams(vmem_limit_bytes=16 * 2**20),
+        scratch_shapes=[
+            pltpu.VMEM((3, 3, 3, CH, CH), BF),
+            pltpu.VMEM((KMID, 2 * CH), BF),
+            pltpu.SemaphoreType.DMA((9,)),
+            pltpu.SemaphoreType.DMA((9,)),
+        ],
+        compiler_params=pltpu.CompilerParams(vmem_limit_bytes=20 * 2**20),
         name="prep",
     )(w_mid)
 
 
-def slots_body(before_ref, own_ref, o_ref, rows, out):
+def slots_body(own_ref, o_ref, rows, out):
     for c in range(3):
         lanes = slice(c * 128, (c + 1) * 128)
-        rows[c, 0:8, :] = before_ref[:, lanes].astype(F32)[HT - 8 : HT]
+        rows[c, 0:8, :] = jnp.zeros((8, 128), F32)
         rows[c, 8 : 8 + HT, :] = own_ref[:, lanes].astype(F32)
         for k in range(8):
             piece = rows[c, 4 + k : 4 + k + HT, :] if k < 5 else jnp.zeros((HT, 128), F32)
@@ -62,30 +81,48 @@
         o_ref[:, :, lanes] = out[c].reshape(HT, 8, 128).astype(BF)
 
 
-def slots(before, own):
+def slots(own):
     return pl.pallas_call(
         slots_body,
         out_shape=jax.ShapeDtypeStruct((HT, 8, CH), BF),
         scratch_shapes=[pltpu.VMEM((3, HT + 8, 128), F32), pltpu.VMEM((3, HT * 8, 128), F32)],
         compiler_params=pltpu.CompilerParams(vmem_limit_bytes=8 * 2**20),
         name="slots",
-    )(before, own)
+    )(own)
+
+
+def patch_body(before_ref, s_ref, o_ref):
+    tail = before_ref[...].astype(F32)[HT - 8 : HT]
+    for d in range(4):
+        here = s_ref[d].astype(F32)
+        o_ref[d] = jnp.concatenate([tail[4 + d : 8], here[4 - d : 8]], axis=0).astype(BF)
+
+
+def patch(before, own_slots):
+    block = pl.BlockSpec((4, 8, CH), lambda n: (0, 0, 0))
+    return pl.pallas_call(
+        patch_body,
+        grid=(1,),
+        in_specs=[pl.BlockSpec((HT, CH), lambda n: (0, 0)), block],
+        out_specs=block,
+        out_shape=jax.ShapeDtypeStruct((HT, 8, CH), BF),
+        input_output_aliases={1: 0},
+        compiler_params=pltpu.CompilerParams(vmem_limit_bytes=8 * 2**20),
+        name="patch",
+    )(before, own_slots)
 
 
 def main_body(
-    pos_ref, len_ref, x_ref, win_ref, bin_ref, bmid_ref, ss_hbm, ds_hbm, sd_hbm, w_hbm, out_hbm,
-    xf, xp, zt, at, hf, hb, dc, dr, dd, w_ss, w_ds, w_sd, w_dd, r_ss, r_ds, r_sd, r_dd, st, ob, wsem, osem,
+    pos_ref, len_ref, x_ref, win_ref, bin_ref, bmid_ref, w_ss, w_ds, sd_hbm, w_hbm, out_hbm,
+    xf, xp, zt, at, hf, hb, dc, dr, dd, w_sd, w_dd, r_ss, r_ds, r_sd, r_dd, st, ob, wsem, osem,
 ):
-    sums = [
-        pltpu.make_async_copy(src, dst, wsem.at[k])
-        for k, (src, dst) in enumerate(((ss_hbm, w_ss), (ds_hbm, w_ds), (sd_hbm, w_sd)))
-    ]
+    row_sums = pltpu.make_async_copy(sd_hbm, w_sd, wsem.at[0])
     outer = [
-        pltpu.make_async_copy(w_hbm.at[t, p, q], w_dd.at[k, pl.ds(t * CH, CH)], wsem.at[3 + 3 * k + t])
+        pltpu.make_async_copy(w_hbm.at[t, p, q], w_dd.at[k, pl.ds(t * CH, CH)], wsem.at[1 + 3 * k + t])
         for k, (p, q) in enumerate(((0, 0), (0, 2), (2, 0), (2, 2)))
         for t in range(3)
     ]
-    for cp in sums + outer:
+    for cp in [row_sums] + outer:
         cp.start()
 
     first = pos_ref[0] - 4
@@ -141,9 +178,7 @@
                 u = times(u * (1.0 + jnp.tanh(u)), m_mid[g]).astype(BF).astype(F32)
                 hf[3 * g + c, pl.ds(TOP + s * SW + j, HT, stride=PITCH), :] = u
 
-    for cp in sums + outer:
-        cp.wait()
-
+    row_sums.wait()
     half = MROW // 2
     for k in range(9):
         lanes = slice(k * 128, (k + 1) * 128)
@@ -166,6 +201,8 @@
     mm(r_ds, dc, HT * PITCH, w_ds[...])
     mm(r_sd, dr, MROW, w_sd[...])
 
+    for cp in outer:
+        cp.wait()
     mm(r_dd, dd, MROW, jnp.concatenate([w_dd[k] for k in range(4)], axis=1))
 
     def emit(i, c):
@@ -198,7 +235,7 @@
     hbm = pl.BlockSpec(memory_space=pl.ANY)
     return pl.pallas_call(
         main_body,
-        in_specs=[smem, smem, vmem, vmem, vmem, vmem, hbm, hbm, hbm, hbm],
+        in_specs=[smem, smem, vmem, vmem, vmem, vmem, vmem, vmem, hbm, hbm],
         out_specs=hbm,
         out_shape=jax.ShapeDtypeStruct((1, 2 * HT, 2 * WT, CH), BF),
         scratch_shapes=[
@@ -211,8 +248,6 @@
             pltpu.VMEM((MROW, KMID), BF),
             pltpu.VMEM((MROW, KMID), BF),
             pltpu.VMEM((MROW, KMID), BF),
-            pltpu.VMEM((KMID, CH), BF),
-            pltpu.VMEM((KMID, 2 * CH), BF),
             pltpu.VMEM((KMID, 2 * CH), BF),
             pltpu.VMEM((4, KMID, CH), BF),
             pltpu.VMEM((3, HT * PITCH, 128), F32),
@@ -221,7 +256,7 @@
             pltpu.VMEM((12, MROW, 128), F32),
             pltpu.VMEM((3, 4, 2, 2 * WT, 128), F32),
             pltpu.VMEM((2 * HT, 2 * WT, CH), BF),
-            pltpu.SemaphoreType.DMA((15,)),
+            pltpu.SemaphoreType.DMA((13,)),
             pltpu.SemaphoreType.DMA,
         ],
         compiler_params=pltpu.CompilerParams(vmem_limit_bytes=VMEM_LIMIT),
@@ -232,11 +267,12 @@
 def on_device(latents, lengths, w_in, b_in, w_mid, b_mid):
     groups = lax.axis_size("req")
     before = lax.ppermute(latents, "req", [(i, i + 1) for i in range(groups - 1)])
-    x = lax.all_to_all(slots(before, latents), "tm", split_axis=0, concat_axis=0, tiled=True)
+    x = lax.all_to_all(patch(before, slots(latents)), "tm", split_axis=0, concat_axis=0, tiled=True)
     w_mid = pltpu.with_memory_space_constraint(w_mid, pltpu.HBM)
-    sums = [pltpu.with_memory_space_constraint(w, pltpu.HBM) for w in prep(w_mid)]
+    ss, ds, sd = prep(w_mid)
+    sd = pltpu.with_memory_space_constraint(sd, pltpu.HBM)
     pos = lax.axis_index(("req", "tm")).astype(jnp.int32).reshape(1)
-    return decode(pos, lengths, x, w_in.reshape(KIN, CH), b_in, b_mid, *sums, w_mid)
+    return decode(pos, lengths, x, w_in.reshape(KIN, CH), b_in, b_mid, ss, ds, sd, w_mid)
 
 
 def solution(mesh):

time: 40.3 us -> 37.7 us (0.935)
  Pallas kernels: 24.4 us -> 19.8 us
  waiting for transfers between devices: 1.14 us -> 3.58 us
    pallas_call x2 -> x3, Pallas kernels: 23.6 us -> 19.1 us  [the longest x1 13.1 us: decode(): pl.pallas_call(main_body, in_specs=[smem, smem, vmem, vmem, vmem, vmem, v...]
    all_to_all x1, waiting for transfers between devices: 0.01 us -> 3.57 us  [on_device(): lax.all_to_all(patch(before, slots(latents)), 'tm', split_axis=0, concat_...]
    ppermute x1, waiting for transfers between devices: 1.14 us -> 0.01 us  [on_device(): lax.ppermute(latents, 'req', [(i, i + 1) for i in range(groups - 1)])]
  transfers between devices with their start and end apart: 2 -> 2, of which waited for: 1 -> 1; matrix products, arithmetic and copies ran while one was open for 0% -> 0% of each run, Pallas kernels for 22% -> 14%
where the time goes in v1:
time: 37.7 us; the launch traced here: 37.3 us
  Pallas kernels  19.8 us (53%)
  starting transfers between devices  13.1 us (35%)
  waiting for transfers between devices  3.58 us (9%)
  local copies, waits for them, and re-layouts  0.77 us (2%)
    pallas_call x1, Pallas kernels, decode(): pl.pallas_call(main_body, in_specs=[smem, smem, vmem, vmem, vmem, vmem, v...  13.1 us
    all_to_all x1, starting transfers between devices, on_device(): lax.all_to_all(patch(before, slots(latents)), 'tm', split_axis=0, concat_...  9.06 us
    pallas_call x1, Pallas kernels, prep(): pl.pallas_call(prep_body, in_specs=[hbm], out_specs=[vmem, vmem, hbm], ou...  4.59 us
    ppermute x1, starting transfers between devices, on_device(): lax.ppermute(latents, 'req', [(i, i + 1) for i in range(groups - 1)])  4.01 us
    all_to_all x1, waiting for transfers between devices, on_device(): lax.all_to_all(patch(before, slots(latents)), 'tm', split_axis=0, concat_...  3.57 us
    pallas_call x1, Pallas kernels, patch(): pl.pallas_call(patch_body, grid=(1,), in_specs=[pl.BlockSpec((HT, CH), la...  1.35 us
    pallas_call x1, Pallas kernels, slots(): pl.pallas_call(slots_body, out_shape=jax.ShapeDtypeStruct((HT, 8, CH), BF...  0.78 us
    unnamed x10, local copies, waits for them, and re-layouts  0.77 us
  transfers between devices with their start and end apart: 2, of which 1 were waited for; matrix products, arithmetic and copies ran while one was open for 0% of the time, Pallas kernels for 14%

profile of v1, /device:TPU:1, one launch (start us, length us, event | category | flops | bytes accessed | tf_op | source)
XLA Modules:
  0.0 37.3 jit_solution(5454703413154600001)
XLA Ops:
  0.0 4.0 %collective-permute-start = (bf16[32,384]{1,0:T(8,128)(2,1)}, bf16[32,384]{1,0:T(8,128)(2,1)S(1)}, u32[]{:S(2)}, u32[]{:S(2)}) collective-permute-start(bf16[32,384]{1,0:T(8,128)(2,1)} %own_ref.1), channel_id=1, source_target_pairs={{0,32},{32,64},{64,96},{1,33},{33,65},{65,97},{2,34},{34,66},{66,9... | collective-permute-start | bytes 73736 | tf_op jit(solution)/shard_map/ppermute | solution.py:269
  4.0 0.0 copy-start.1
  4.0 0.7 %copy-done.1 = bf16[32,384]{1,0:T(8,128)(2,1)S(1)} copy-done((bf16[32,384]{1,0:T(8,128)(2,1)S(1)}, bf16[32,384]{1,0:T(8,128)(2,1)}, u32[]{:S(2)}) %copy-start.1) | copy-done | bytes 24600
  4.8 0.8 %slots.1.s_ref = bf16[32,8,384]{2,1,0:T(8,128)(2,1)} custom-call(bf16[32,384]{1,0:T(8,128)(2,1)S(1)} %copy-done.1), custom_call_target="tpu_custom_call" | custom-call | tf_op jit(solution)/shard_map/slots/pallas_call | solution.py:85
  5.5 0.0 collective-permute-done.before_ref
  5.6 1.4 %patch.1 = bf16[32,8,384]{2,1,0:T(8,128)(2,1)} custom-call(bf16[32,384]{1,0:T(8,128)(2,1)S(1)} %collective-permute-done.before_ref, bf16[32,8,384]{2,1,0:T(8,128)(2,1)} %slots.1.s_ref), custom_call_target="tpu_custom_call", output_to_operand_aliasing={{}: (1, {})} | custom-call | tf_op jit(solution)/shard_map/patch/pallas_call | solution.py:103
  6.9 9.1 %all-to-all-start = ((bf16[32,8,384]{2,1,0:T(8,128)(2,1)}), bf16[32,8,384]{2,1,0:T(8,128)(2,1)S(1)}, u32[]{:S(2)}, u32[]{:S(2)}) async-start(bf16[32,8,384]{2,1,0:T(8,128)(2,1)} %patch.1), calls=%async_computation | async-start | bytes 393216 | tf_op jit(solution)/shard_map/all_to_all | solution.py:270
  16.0 0.0 copy-start
  16.0 0.0 copy-start.2
  16.0 0.0 copy-start.3
  16.0 0.0 copy-start.4
  16.0 4.6 %prep.1 = (bf16[1152,384]{1,0:T(8,128)(2,1)S(1)}, bf16[1152,768]{1,0:T(8,128)(2,1)S(1)}, bf16[1152,768]{1,0:T(8,128)(2,1)}) custom-call(bf16[3,3,3,384,384]{4,3,2,1,0:T(8,128)(2,1)} %w_hbm.3), custom_call_target="tpu_custom_call" | custom-call | tf_op jit(solution)/shard_map/prep/pallas_call | solution.py:53
  20.6 3.6 %all-to-all-done.x_ref = bf16[32,8,384]{2,1,0:T(8,128)(2,1)S(1)} async-done(((bf16[32,8,384]{2,1,0:T(8,128)(2,1)}), bf16[32,8,384]{2,1,0:T(8,128)(2,1)S(1)}, u32[]{:S(2)}, u32[]{:S(2)}) %all-to-all-start) | async-done | bytes 196640 | tf_op jit(solution)/shard_map/all_to_all | solution.py:270
  24.2 0.0 copy-done
  24.2 0.0 copy-done.2
  24.2 0.0 copy-done.3
  24.2 0.0 copy-done.4
  24.2 13.1 %decode.1 = bf16[1,64,48,384]{3,2,1,0:T(8,128)(2,1)} custom-call(s32[1]{0:T(128)} %bitcast.pos_ref, s32[8]{0:T(128)S(1)} %copy-done.4, bf16[32,8,384]{2,1,0:T(8,128)(2,1)S(1)} %all-to-all-done.x_ref, bf16[432,384]{1,0:T(8,128)(2,1)S(1)} %bitcast.2, f32[384]{0:T(512)S(1)} %copy-done.2, f32[384]{0:T(512)S(1)} %copy-done.3, ...), custom_call_target="tpu_custom_call" | custom-call | tf_op jit(solution)/shard_map/decode/pallas_call | solution.py:236
Async XLA Ops:
  0.0 5.5 %collective-permute-start = (bf16[32,384]{1,0:T(8,128)(2,1)}, bf16[32,384]{1,0:T(8,128)(2,1)S(1)}, u32[]{:S(2)}, u32[]{:S(2)}) collective-permute-start(bf16[32,384]{1,0:T(8,128)(2,1)} %own_ref.1), channel_id=1, source_target_pairs={{0,32},{32,64},{64,96},{1,33},{33,65},{65,97},{2,34},{34,66},{66,9... | collective-permute-start | bytes 73736 | tf_op jit(solution)/shard_map/ppermute | solution.py:269
  4.0 0.8 %copy-start.1 = (bf16[32,384]{1,0:T(8,128)(2,1)S(1)}, bf16[32,384]{1,0:T(8,128)(2,1)}, u32[]{:S(2)}) copy-start(bf16[32,384]{1,0:T(8,128)(2,1)} %own_ref.1) | copy-start | bytes 73732
  6.9 17.3 %all-to-all-start = ((bf16[32,8,384]{2,1,0:T(8,128)(2,1)}), bf16[32,8,384]{2,1,0:T(8,128)(2,1)S(1)}, u32[]{:S(2)}, u32[]{:S(2)}) async-start(bf16[32,8,384]{2,1,0:T(8,128)(2,1)} %patch.1), calls=%async_computation | async-start | bytes 393216 | tf_op jit(solution)/shard_map/all_to_all | solution.py:270
  16.0 8.2 %copy-start = (bf16[3,3,3,16,384]{4,3,2,1,0:T(8,128)(2,1)S(1)}, bf16[3,3,3,16,384]{4,3,2,1,0:T(8,128)(2,1)}, u32[]{:S(2)}) copy-start(bf16[3,3,3,16,384]{4,3,2,1,0:T(8,128)(2,1)} %param.8) | copy-start | bytes 995332
  16.0 8.2 %copy-start.2 = (f32[384]{0:T(512)S(1)}, f32[384]{0:T(512)}, u32[]{:S(2)}) copy-start(f32[384]{0:T(512)} %bin_ref.1) | copy-start | bytes 4612
  16.0 8.2 %copy-start.3 = (f32[384]{0:T(512)S(1)}, f32[384]{0:T(512)}, u32[]{:S(2)}) copy-start(f32[384]{0:T(512)} %bmid_ref.1) | copy-start | bytes 4612
  16.0 8.2 %copy-start.4 = (s32[8]{0:T(128)S(1)}, s32[8]{0:T(128)}, u32[]{:S(2)}) copy-start(s32[8]{0:T(128)} %len_ref.1) | copy-start | bytes 100

commit v2 on v1

v2 whole, which is shorter than its diff:
```python
import jax
import jax.numpy as jnp
from jax import lax
from jax.experimental import pallas as pl
from jax.experimental.pallas import tpu as pltpu
from jax.sharding import PartitionSpec as P

C = 16
HT = 32
WT = 24
CH = 384
BF = jnp.bfloat16
F32 = jnp.float32
KIN = 27 * C
KMID = 3 * CH
STRIP = 4
SW = WT // STRIP
VMEM_LIMIT = 44 * 2**20
PITCH = WT + 1
TOP = 32
HALF = HT // 2
FULL = HALF * PITCH
MORE = 432


def prep_body(w_hbm, ss_ref, sd_ref, by_col_hbm, mixed_hbm, w, by_col, mixed, isem, osem):
    rows = 128
    parts = [(t, slice(r, r + rows)) for t in range(3) for r in range(0, CH, rows)]
    reads, writes = [], []
    for n, (t, r) in enumerate(parts):
        cp = pltpu.make_async_copy(w_hbm.at[t, :, :, r], w.at[t, :, :, r], isem.at[n])
        cp.start()
        reads.append(cp)
    for n, (t, r) in enumerate(parts):
        reads[n].wait()
        out = slice(n * rows, (n + 1) * rows)
        row = [[w[t, p, q, r].astype(F32) for q in range(3)] for p in range(3)]
        cols = [[x[0] + x[1] + x[2] for x in row], [x[0] for x in row], [x[2] for x in row]]
        for k, (x, y, z) in enumerate(cols):
            upper, lower = x + y, y + z
            whole = (upper + z).astype(BF)
            if k == 0:
                ss_ref[out] = whole
                by_col[0, out, 0:CH] = x.astype(BF)
                by_col[0, out, CH : 2 * CH] = upper.astype(BF)
                by_col[1, out, 0:CH] = lower.astype(BF)
                by_col[1, out, CH : 2 * CH] = z.astype(BF)
            else:
                sd_ref[out, (k - 1) * CH : k * CH] = whole
                mixed[k - 1, out] = upper.astype(BF)
                mixed[k + 1, out] = lower.astype(BF)
        for k, (src, dst) in enumerate(((by_col, by_col_hbm), (mixed, mixed_hbm))):
            cp = pltpu.make_async_copy(src.at[:, out], dst.at[:, out], osem.at[k, n])
            cp.start()
            writes.append(cp)
    for cp in writes:
        cp.wait()


def prep(w_mid):
    vmem = pl.BlockSpec(memory_space=pltpu.VMEM)
    hbm = pl.BlockSpec(memory_space=pl.ANY)
    return pl.pallas_call(
        prep_body,
        in_specs=[hbm],
        out_specs=[vmem, vmem, hbm, hbm],
        out_shape=[
            jax.ShapeDtypeStruct((KMID, CH), BF),
            jax.ShapeDtypeStruct((KMID, 2 * CH), BF),
            pltpu.HBM((2, KMID, 2 * CH), BF),
            pltpu.HBM((4, KMID, CH), BF),
        ],
        scratch_shapes=[
            pltpu.VMEM((3, 3, 3, CH, CH), BF),
            pltpu.VMEM((2, KMID, 2 * CH), BF),
            pltpu.VMEM((4, KMID, CH), BF),
            pltpu.SemaphoreType.DMA((9,)),
            pltpu.SemaphoreType.DMA((2, 9)),
        ],
        compiler_params=pltpu.CompilerParams(vmem_limit_bytes=24 * 2**20),
        name="prep",
    )(w_mid)


def slots_body(own_ref, o_ref, rows, out):
    for c in range(3):
        lanes = slice(c * 128, (c + 1) * 128)
        rows[c, 0:8, :] = jnp.zeros((8, 128), F32)
        rows[c, 8 : 8 + HT, :] = own_ref[:, lanes].astype(F32)
        for k in range(8):
            piece = rows[c, 4 + k : 4 + k + HT, :] if k < 5 else jnp.zeros((HT, 128), F32)
            out[c, pl.ds(k, HT, stride=8), :] = piece
        o_ref[:, :, lanes] = out[c].reshape(HT, 8, 128).astype(BF)


def slots(own):
    return pl.pallas_call(
        slots_body,
        out_shape=jax.ShapeDtypeStruct((HT, 8, CH), BF),
        scratch_shapes=[pltpu.VMEM((3, HT + 8, 128), F32), pltpu.VMEM((3, HT * 8, 128), F32)],
        compiler_params=pltpu.CompilerParams(vmem_limit_bytes=8 * 2**20),
        name="slots",
    )(own)


def patch_body(before_ref, s_ref, o_ref):
    o_ref[4:HT] = s_ref[4:HT]
    tail = before_ref[...].astype(F32)[HT - 8 : HT]
    for d in range(4):
        here = s_ref[d].astype(F32)
        o_ref[d] = jnp.concatenate([tail[4 + d : 8], here[4 - d : 8]], axis=0).astype(BF)


def patch(before, own_slots):
    return pl.pallas_call(
        patch_body,
        out_shape=jax.ShapeDtypeStruct((HT, 8, CH), BF),
        compiler_params=pltpu.CompilerParams(vmem_limit_bytes=8 * 2**20),
        name="patch",
    )(before, own_slots)


def main_body(
    pos_ref, len_ref, x_ref, win_ref, bin_ref, bmid_ref, w_ss, w_sd, by_col_hbm, mixed_hbm,
    w_hbm, out_hbm, xf, xp, zt, at, even, odd, ls, lsd, lm, lmd, lp, lpd, w_by_col, w_m, w_p,
    r_ss, r_sd, r_ms, r_md, r_ps, r_pd, st, ob, wsem, osem,
):
    copy = pltpu.make_async_copy
    by_col = [copy(by_col_hbm.at[k], w_by_col.at[k], wsem.at[k]) for k in range(2)]
    both = []
    for k, (w, p) in enumerate(((w_m, 0), (w_p, 2))):
        for q in range(2):
            both.append(copy(mixed_hbm.at[2 * k + q], w.at[2 - p + q], wsem.at[2 + 2 * k + q]))
            for t in range(3):
                part = pl.ds(t * CH, CH)
                both.append(
                    copy(w_hbm.at[t, p, 2 * q], w.at[p + q, part], wsem.at[6 + 6 * k + 3 * q + t])
                )
    for cp in by_col:
        cp.start()

    first = pos_ref[0] - 4
    rid = [jnp.int32(0)] * 5
    end = jnp.int32(0)
    for r in range(8):
        end = end + len_ref[r]
        rid = [rid[k] + (first + k >= end).astype(jnp.int32) for k in range(5)]
    ok = lambda k, g: ((first + k >= 0) & (rid[k] == rid[g])).astype(F32)
    m_in = [[ok(g + t, g + 2) if t < 2 else None for t in range(3)] for g in range(3)]
    m_mid = [ok(2, 4), ok(3, 4), None]
    bias = lambda ref, c: ref[pl.ds(c * 128, 128)].reshape(1, 128)
    times = lambda v, m: v if m is None else v * m

    for c in range(3):
        xf[c] = x_ref[:, :, c * 128 : (c + 1) * 128].reshape(HT * 8, 128).astype(F32)
    for f in range(5):
        x = [0.5 * xf[c, pl.ds(f, HT, stride=8), :] for c in range(3)]
        x = jnp.concatenate([jnp.zeros((HT, C), F32)] + x + [jnp.zeros((HT, 128 - C), F32)], axis=1)
        for s in range(STRIP):
            k = f * STRIP + s
            xp[k, 0:8, :] = jnp.zeros((8, 128), F32)
            xp[k, 8 : 8 + HT, :] = x[:, s * SW * C : s * SW * C + 128]
            xp[k, 8 + HT : 16 + HT, :] = jnp.zeros((8, 128), F32)

    for t in range(3):
        for p in range(3):
            for b in range(3):
                block = []
                for k in range(4 * b, 4 * b + 4):
                    s, g = k // 3, k % 3
                    for first_row in (7 + p, 8 + p):
                        x = xp[(g + t) * STRIP + s, pl.ds(first_row, HALF, stride=2), :]
                        block.append(times(x, m_in[g][t]).astype(BF))
                z = jnp.concatenate(block, axis=0)
                zt[3 * t + p, :, b * 128 : (b + 1) * 128] = z.T

    for tp in range(9):
        for j in range(SW):
            at[tp * 48 : (tp + 1) * 48, j * CH : (j + 1) * CH] = zt[tp, 16 * j : 16 * j + 48, :]

    for k in range(9):
        for ref in (even, odd):
            ref[k, 0:TOP, :] = jnp.zeros((TOP, 128), F32)
            ref[k, pl.ds(TOP + WT, HALF, stride=PITCH), :] = jnp.zeros((HALF, 128), F32)
            ref[k, TOP + FULL : TOP + MORE, :] = jnp.zeros((MORE - FULL, 128), F32)

    for cp in both:
        cp.start()
    for n in range(SW // 2):
        a = at[:, n * 2 * CH : (n + 1) * 2 * CH]
        v = lax.dot_general(a, win_ref[...], (((0,), (0,)), ((), ())), preferred_element_type=F32)
        for k in range(2 * STRIP * 3):
            s, g, j = k // 3 % STRIP, k % 3, n * 2 + k // (3 * STRIP)
            for c in range(3):
                u = v[k * HT : (k + 1) * HT, c * 128 : (c + 1) * 128]
                u = u + 0.5 * bias(bin_ref, c)
                u = times(u * (1.0 + jnp.tanh(u)), m_mid[g]).astype(BF).astype(F32)
                to = pl.ds(TOP + s * SW + j, HALF, stride=PITCH)
                even[3 * g + c, to, :] = u[0:HALF]
                odd[3 * g + c, to, :] = u[HALF:HT]

    for cp in by_col:
        cp.wait()

    def build(plain, diff, value, rows, step):
        for k in range(9):
            lanes = slice(k * 128, (k + 1) * 128)
            for lo in range(0, rows, step):
                to = slice(lo, lo + step)
                here = value(k, lo, step)
                plain[to, lanes] = here.astype(BF)
                diff[to, lanes] = (here - value(k, lo - 1, step)).astype(BF)

    on_even = lambda k, lo, n: even[k, TOP + lo : TOP + lo + n, :]
    below = lambda k, lo, n: odd[k, TOP + lo : TOP + lo + n, :]
    def mm(out, first_chunk, lhs, w):
        v = jnp.dot(lhs[...], w, preferred_element_type=F32)
        for k in range(v.shape[1] // 128):
            part = v[:, k * 128 : (k + 1) * 128]
            out[first_chunk + k] = part + bias(bmid_ref, k) if out is r_ss else part

    build(ls, lsd, on_even, FULL, 80)
    mm(r_ss, 0, ls, w_ss[...])
    mm(r_sd, 0, lsd, w_sd[...])
    build(lm, lmd, lambda k, lo, n: below(k, lo - PITCH, n) - on_even(k, lo, n), MORE, 144)
    mm(r_ms, 0, lm, w_by_col[0])
    build(lp, lpd, lambda k, lo, n: below(k, lo, n) - on_even(k, lo, n), FULL, 80)
    mm(r_ps, 0, lp, w_by_col[1])
    for cp in both:
        cp.wait()

    def emit(m, c):
        at_row = lambda ref, k, off: ref[k, m * PITCH + off : m * PITCH + off + WT, :]
        slot = m % 4

        def columns(plain, diff, k):
            x = at_row(plain, 3 * k + c, 0)
            return x - at_row(diff, 4 * c + 2 * k, 0), x + at_row(diff, 4 * c + 2 * k + 1, 1)

        if m < HALF:
            x = at_row(r_ss, c, 0)
            base = x - at_row(r_sd, c, 0), x + at_row(r_sd, 3 + c, 1)
        else:
            base = bias(bmid_ref, c), bias(bmid_ref, c)
        rows = {4 * m - 1: (r_ms, r_md, 1), 4 * m: (r_ms, r_md, 0)}
        rows.update({4 * m + 1: (r_ps, r_pd, 1), 4 * m + 2: (r_ps, r_pd, 0)})
        for n, (u, (plain, diff, k)) in enumerate(rows.items()):
            if 0 <= u < 2 * HT and (m < HALF or n == 0):
                y = columns(plain, diff, k)
                for b in range(2):
                    st[c, slot, n, pl.ds(b, WT, stride=2), :] = base[b] + y[b]
                ob[u, :, c * 128 : (c + 1) * 128] = st[c, slot, n].astype(BF)

    def diff_part(c):
        for out, lhs, w in ((r_md, lmd, w_m), (r_pd, lpd, w_p)):
            weights = [w[k, :, c * 128 : (c + 1) * 128] for k in range(4)]
            mm(out, 4 * c, lhs, jnp.concatenate(weights, axis=1))

    def out_part(c):
        for m in range(HALF + 1):
            emit(m, c)
            if c == 2 and m % 4 == 0 and m > 0:
                block = pl.ds(4 * m - 16, 16)
                pltpu.make_async_copy(ob.at[block], out_hbm.at[0, block], osem).start()

    diff_part(0)
    diff_part(1)
    out_part(0)
    diff_part(2)
    out_part(1)
    out_part(2)
    pltpu.make_async_copy(ob, out_hbm.at[0], osem).wait()


def decode(pos, lengths, x, w_in, b_in, b_mid, ss, sd, by_col, mixed, w_mid):
    smem = pl.BlockSpec(memory_space=pltpu.SMEM)
    vmem = pl.BlockSpec(memory_space=pltpu.VMEM)
    hbm = pl.BlockSpec(memory_space=pl.ANY)
    return pl.pallas_call(
        main_body,
        in_specs=[smem, smem, vmem, vmem, vmem, vmem, vmem, vmem, hbm, hbm, hbm],
        out_specs=hbm,
        out_shape=jax.ShapeDtypeStruct((1, 2 * HT, 2 * WT, CH), BF),
        scratch_shapes=[
            pltpu.VMEM((3, HT * 8, 128), F32),
            pltpu.VMEM((5 * STRIP, HT + 16, 128), F32),
            pltpu.VMEM((9, 128, CH), BF),
            pltpu.VMEM((KIN, SW * CH), BF),
            pltpu.VMEM((9, TOP + MORE, 128), F32),
            pltpu.VMEM((9, TOP + MORE, 128), F32),
            pltpu.VMEM((FULL, KMID), BF),
            pltpu.VMEM((FULL, KMID), BF),
            pltpu.VMEM((MORE, KMID), BF),
            pltpu.VMEM((MORE, KMID), BF),
            pltpu.VMEM((FULL, KMID), BF),
            pltpu.VMEM((FULL, KMID), BF),
            pltpu.VMEM((2, KMID, 2 * CH), BF),
            pltpu.VMEM((4, KMID, CH), BF),
            pltpu.VMEM((4, KMID, CH), BF),
            pltpu.VMEM((3, FULL, 128), F32),
            pltpu.VMEM((6, FULL, 128), F32),
            pltpu.VMEM((6, MORE, 128), F32),
            pltpu.VMEM((12, MORE, 128), F32),
            pltpu.VMEM((6, FULL, 128), F32),
            pltpu.VMEM((12, FULL, 128), F32),
            pltpu.VMEM((3, 4, 4, 2 * WT, 128), F32),
            pltpu.VMEM((2 * HT, 2 * WT, CH), BF),
            pltpu.SemaphoreType.DMA((18,)),
            pltpu.SemaphoreType.DMA,
        ],
        compiler_params=pltpu.CompilerParams(vmem_limit_bytes=VMEM_LIMIT),
        name="decode",
    )(pos, lengths, x, w_in, b_in, b_mid, ss, sd, by_col, mixed, w_mid)


def on_device(latents, lengths, w_in, b_in, w_mid, b_mid):
    groups = lax.axis_size("req")
    before = lax.ppermute(latents, "req", [(i, i + 1) for i in range(groups - 1)])
    x = lax.all_to_all(patch(before, slots(latents)), "tm", split_axis=0, concat_axis=0, tiled=True)
    w_mid = pltpu.with_memory_space_constraint(w_mid, pltpu.HBM)
    ss, sd, by_col, mixed = prep(w_mid)
    by_col = pltpu.with_memory_space_constraint(by_col, pltpu.HBM)
    mixed = pltpu.with_memory_space_constraint(mixed, pltpu.HBM)
    pos = lax.axis_index(("req", "tm")).astype(jnp.int32).reshape(1)
    return decode(pos, lengths, x, w_in.reshape(KIN, CH), b_in, b_mid, ss, sd, by_col, mixed, w_mid)


def solution(mesh):
    in_specs = (P("req", "tm"), P(), P(), P(), P(), P())
    out_specs = P(("req", "tm"), None, None, None)
    return jax.shard_map(
        on_device, mesh=mesh, in_specs=in_specs, out_specs=out_specs, check_vma=False
    )
```

time: 37.7 us -> 36.2 us (0.960)
  waiting for transfers between devices: 3.58 us -> 2.05 us
  starting transfers between devices: 13.1 us -> 13.5 us
    all_to_all x1, waiting for transfers between devices: 3.57 us -> 1.77 us  [on_device(): lax.all_to_all(patch(before, slots(latents)), 'tm', split_axis=0, concat_...]
    pallas_call x2, Pallas kernels: 5.95 us -> 7.1 us  [the longest x1 6.4 us: prep(): pl.pallas_call(prep_body, in_specs=[hbm], out_specs=[vmem, vmem, hbm, hbm...]
    pallas_call x1, Pallas kernels: 13.1 us -> 12.3 us  [decode(): pl.pallas_call(main_body, in_specs=[smem, smem, vmem, vmem, vmem, vmem, v...]
    pallas_call x1, Pallas kernels: 0.78 us -> 0.1 us  [slots(): pl.pallas_call(slots_body, out_shape=jax.ShapeDtypeStruct((HT, 8, CH), BF...]
    all_to_all x1, starting transfers between devices: 9.06 us -> 9.46 us  [on_device(): lax.all_to_all(patch(before, slots(latents)), 'tm', split_axis=0, concat_...]
  transfers between devices with their start and end apart: 2 -> 2, of which waited for: 1 -> 2; matrix products, arithmetic and copies ran while one was open for 0% -> 0% of each run, Pallas kernels for 14% -> 18%
where the time goes in v2:
time: 36.2 us; the launch traced here: 35.9 us
  Pallas kernels  19.5 us (54%)
  starting transfers between devices  13.5 us (37%)
  waiting for transfers between devices  2.05 us (6%)
  local copies, waits for them, and re-layouts  0.77 us (2%)
    pallas_call x1, Pallas kernels, decode(): pl.pallas_call(main_body, in_specs=[smem, smem, vmem, vmem, vmem, vmem, v...  12.3 us
    all_to_all x1, starting transfers between devices, on_device(): lax.all_to_all(patch(before, slots(latents)), 'tm', split_axis=0, concat_...  9.46 us
    pallas_call x1, Pallas kernels, prep(): pl.pallas_call(prep_body, in_specs=[hbm], out_specs=[vmem, vmem, hbm, hbm...  6.4 us
    ppermute x1, starting transfers between devices, on_device(): lax.ppermute(latents, 'req', [(i, i + 1) for i in range(groups - 1)])  4.01 us
    all_to_all x1, waiting for transfers between devices, on_device(): lax.all_to_all(patch(before, slots(latents)), 'tm', split_axis=0, concat_...  1.77 us
    unnamed x10, local copies, waits for them, and re-layouts  0.77 us
  transfers between devices with their start and end apart: 2, of which 2 were waited for; matrix products, arithmetic and copies ran while one was open for 0% of the time, Pallas kernels for 18%

profile of v2, /device:TPU:1, one launch (start us, length us, event | category | flops | bytes accessed | tf_op | source)
XLA Modules:
  0.0 35.9 jit_solution(10012460559547560818)
XLA Ops:
  0.0 4.0 %collective-permute-start = (bf16[32,384]{1,0:T(8,128)(2,1)}, bf16[32,384]{1,0:T(8,128)(2,1)S(1)}, u32[]{:S(2)}, u32[]{:S(2)}) collective-permute-start(bf16[32,384]{1,0:T(8,128)(2,1)} %own_ref.1), channel_id=1, source_target_pairs={{0,32},{32,64},{64,96},{1,33},{33,65},{65,97},{2,34},{34,66},{66,9... | collective-permute-start | bytes 73736 | tf_op jit(solution)/shard_map/ppermute | solution.py:318
  4.0 0.0 copy-start.1
  4.0 0.7 %copy-done.1 = bf16[32,384]{1,0:T(8,128)(2,1)S(1)} copy-done((bf16[32,384]{1,0:T(8,128)(2,1)S(1)}, bf16[32,384]{1,0:T(8,128)(2,1)}, u32[]{:S(2)}) %copy-start.1) | copy-done | bytes 24600
  4.8 0.1 slots.1.s_ref
  4.9 0.3 collective-permute-done.before_ref
  5.2 0.7 %patch.1 = bf16[32,8,384]{2,1,0:T(8,128)(2,1)} custom-call(bf16[32,384]{1,0:T(8,128)(2,1)S(1)} %collective-permute-done.before_ref, bf16[32,8,384]{2,1,0:T(8,128)(2,1)S(1)} %slots.1.s_ref), custom_call_target="tpu_custom_call" | custom-call | tf_op jit(solution)/shard_map/patch/pallas_call | solution.py:115
  5.9 9.5 %all-to-all-start = ((bf16[32,8,384]{2,1,0:T(8,128)(2,1)}), bf16[32,8,384]{2,1,0:T(8,128)(2,1)S(1)}, u32[]{:S(2)}, u32[]{:S(2)}) async-start(bf16[32,8,384]{2,1,0:T(8,128)(2,1)} %patch.1), calls=%async_computation | async-start | bytes 393216 | tf_op jit(solution)/shard_map/all_to_all | solution.py:319
  15.3 0.0 copy-start
  15.3 0.0 copy-start.2
  15.3 0.0 copy-start.3
  15.4 0.0 copy-start.4
  15.4 6.4 %prep.1 = (bf16[1152,384]{1,0:T(8,128)(2,1)S(1)}, bf16[1152,768]{1,0:T(8,128)(2,1)S(1)}, bf16[2,1152,768]{2,1,0:T(8,128)(2,1)}, bf16[4,1152,384]{2,1,0:T(8,128)(2,1)}) custom-call(bf16[3,3,3,384,384]{4,3,2,1,0:T(8,128)(2,1)} %w_hbm.3), custom_call_target="tpu_custom_call" | custom-call | tf_op jit(solution)/shard_map/prep/pallas_call | solution.py:63
  21.8 1.8 %all-to-all-done.x_ref = bf16[32,8,384]{2,1,0:T(8,128)(2,1)S(1)} async-done(((bf16[32,8,384]{2,1,0:T(8,128)(2,1)}), bf16[32,8,384]{2,1,0:T(8,128)(2,1)S(1)}, u32[]{:S(2)}, u32[]{:S(2)}) %all-to-all-start) | async-done | bytes 196640 | tf_op jit(solution)/shard_map/all_to_all | solution.py:319
  23.6 0.0 copy-done
  23.6 0.0 copy-done.2
  23.6 0.0 copy-done.3
  23.6 0.0 copy-done.4
  23.6 12.3 %decode.1 = bf16[1,64,48,384]{3,2,1,0:T(8,128)(2,1)} custom-call(s32[1]{0:T(128)} %bitcast.pos_ref, s32[8]{0:T(128)S(1)} %copy-done.4, bf16[32,8,384]{2,1,0:T(8,128)(2,1)S(1)} %all-to-all-done.x_ref, bf16[432,384]{1,0:T(8,128)(2,1)S(1)} %bitcast.2, f32[384]{0:T(512)S(1)} %copy-done.2, f32[384]{0:T(512)S(1)} %copy-done.3, ...), custom_call_target="tpu_custom_call" | custom-call | tf_op jit(solution)/shard_map/decode/pallas_call | solution.py:279
Async XLA Ops:
  0.0 5.2 %collective-permute-start = (bf16[32,384]{1,0:T(8,128)(2,1)}, bf16[32,384]{1,0:T(8,128)(2,1)S(1)}, u32[]{:S(2)}, u32[]{:S(2)}) collective-permute-start(bf16[32,384]{1,0:T(8,128)(2,1)} %own_ref.1), channel_id=1, source_target_pairs={{0,32},{32,64},{64,96},{1,33},{33,65},{65,97},{2,34},{34,66},{66,9... | collective-permute-start | bytes 73736 | tf_op jit(solution)/shard_map/ppermute | solution.py:318
  4.0 0.8 %copy-start.1 = (bf16[32,384]{1,0:T(8,128)(2,1)S(1)}, bf16[32,384]{1,0:T(8,128)(2,1)}, u32[]{:S(2)}) copy-start(bf16[32,384]{1,0:T(8,128)(2,1)} %own_ref.1) | copy-start | bytes 73732
  5.9 17.7 %all-to-all-start = ((bf16[32,8,384]{2,1,0:T(8,128)(2,1)}), bf16[32,8,384]{2,1,0:T(8,128)(2,1)S(1)}, u32[]{:S(2)}, u32[]{:S(2)}) async-start(bf16[32,8,384]{2,1,0:T(8,128)(2,1)} %patch.1), calls=%async_computation | async-start | bytes 393216 | tf_op jit(solution)/shard_map/all_to_all | solution.py:319
  15.3 8.2 %copy-start = (bf16[3,3,3,16,384]{4,3,2,1,0:T(8,128)(2,1)S(1)}, bf16[3,3,3,16,384]{4,3,2,1,0:T(8,128)(2,1)}, u32[]{:S(2)}) copy-start(bf16[3,3,3,16,384]{4,3,2,1,0:T(8,128)(2,1)} %param.8) | copy-start | bytes 995332
  15.3 8.2 %copy-start.2 = (f32[384]{0:T(512)S(1)}, f32[384]{0:T(512)}, u32[]{:S(2)}) copy-start(f32[384]{0:T(512)} %bin_ref.1) | copy-start | bytes 4612
  15.3 8.2 %copy-start.3 = (f32[384]{0:T(512)S(1)}, f32[384]{0:T(512)}, u32[]{:S(2)}) copy-start(f32[384]{0:T(512)} %bmid_ref.1) | copy-start | bytes 4612
  15.4 8.2 %copy-start.4 = (s32[8]{0:T(128)S(1)}, s32[8]{0:T(128)}, u32[]{:S(2)}) copy-start(s32[8]{0:T(128)} %len_ref.1) | copy-start | bytes 100

commit v3 on v2

--- a/solution.py
+++ b/solution.py
@@ -13,8 +13,9 @@
 F32 = jnp.float32
 KIN = 27 * C
 KMID = 3 * CH
-STRIP = 4
-SW = WT // STRIP
+WINDOWS = 14
+KPAIR = 640
+GROUP = 3
 VMEM_LIMIT = 44 * 2**20
 PITCH = WT + 1
 TOP = 32
@@ -122,7 +123,7 @@
 
 def main_body(
     pos_ref, len_ref, x_ref, win_ref, bin_ref, bmid_ref, w_ss, w_sd, by_col_hbm, mixed_hbm,
-    w_hbm, out_hbm, xf, xp, zt, at, even, odd, ls, lsd, lm, lmd, lp, lpd, w_by_col, w_m, w_p,
+    w_hbm, out_hbm, xf, xp, wb, at, even, odd, ls, lsd, lm, lmd, lp, lpd, w_by_col, w_m, w_p,
     r_ss, r_sd, r_ms, r_md, r_ps, r_pd, st, ob, wsem, osem,
 ):
     copy = pltpu.make_async_copy
@@ -155,28 +156,22 @@
         xf[c] = x_ref[:, :, c * 128 : (c + 1) * 128].reshape(HT * 8, 128).astype(F32)
     for f in range(5):
         x = [0.5 * xf[c, pl.ds(f, HT, stride=8), :] for c in range(3)]
-        x = jnp.concatenate([jnp.zeros((HT, C), F32)] + x + [jnp.zeros((HT, 128 - C), F32)], axis=1)
-        for s in range(STRIP):
-            k = f * STRIP + s
+        left, right = jnp.zeros((HT, 64 + C), F32), jnp.zeros((HT, 160 + C), F32)
+        x = jnp.concatenate([left] + x + [right], axis=1)
+        for n in range(WINDOWS):
+            k = f * WINDOWS + n
             xp[k, 0:8, :] = jnp.zeros((8, 128), F32)
-            xp[k, 8 : 8 + HT, :] = x[:, s * SW * C : s * SW * C + 128]
+            xp[k, 8 : 8 + HT, :] = x[:, 32 * n : 32 * n + 128]
             xp[k, 8 + HT : 16 + HT, :] = jnp.zeros((8, 128), F32)
 
-    for t in range(3):
-        for p in range(3):
-            for b in range(3):
-                block = []
-                for k in range(4 * b, 4 * b + 4):
-                    s, g = k // 3, k % 3
-                    for first_row in (7 + p, 8 + p):
-                        x = xp[(g + t) * STRIP + s, pl.ds(first_row, HALF, stride=2), :]
-                        block.append(times(x, m_in[g][t]).astype(BF))
-                z = jnp.concatenate(block, axis=0)
-                zt[3 * t + p, :, b * 128 : (b + 1) * 128] = z.T
-
+    wb[...] = jnp.zeros((KPAIR, 2 * CH), BF)
     for tp in range(9):
-        for j in range(SW):
-            at[tp * 48 : (tp + 1) * 48, j * CH : (j + 1) * CH] = zt[tp, 16 * j : 16 * j + 48, :]
+        taps = win_ref[tp * 48 : (tp + 1) * 48, :]
+        wb[tp * 64 : tp * 64 + 48, 0:CH] = taps
+        wb[tp * 64 + 16 : tp * 64 + 64, CH : 2 * CH] = taps
+
+    for cp in both:
+        cp.start()
 
     for k in range(9):
         for ref in (even, odd):
@@ -184,20 +179,42 @@
             ref[k, pl.ds(TOP + WT, HALF, stride=PITCH), :] = jnp.zeros((HALF, 128), F32)
             ref[k, TOP + FULL : TOP + MORE, :] = jnp.zeros((MORE - FULL, 128), F32)
 
-    for cp in both:
-        cp.start()
-    for n in range(SW // 2):
-        a = at[:, n * 2 * CH : (n + 1) * 2 * CH]
-        v = lax.dot_general(a, win_ref[...], (((0,), (0,)), ((), ())), preferred_element_type=F32)
-        for k in range(2 * STRIP * 3):
-            s, g, j = k // 3 % STRIP, k % 3, n * 2 + k // (3 * STRIP)
-            for c in range(3):
-                u = v[k * HT : (k + 1) * HT, c * 128 : (c + 1) * 128]
-                u = u + 0.5 * bias(bin_ref, c)
-                u = times(u * (1.0 + jnp.tanh(u)), m_mid[g]).astype(BF).astype(F32)
-                to = pl.ds(TOP + s * SW + j, HALF, stride=PITCH)
-                even[3 * g + c, to, :] = u[0:HALF]
-                odd[3 * g + c, to, :] = u[HALF:HT]
+    low = lax.broadcasted_iota(jnp.int32, (1, 128), 1) < 64
+    scale = lambda m: jnp.float32(1) if m is None else m
+    mask = [
+        [
+            jnp.where(low, scale(m_in[g][2 * n // 3]), scale(m_in[g][(2 * n + 1) // 3]) if n < 4 else 0.0)
+            for n in range(5)
+        ]
+        for g in range(3)
+    ]
+
+    def window(tp, g, s, par, n):
+        t, p = tp // 3, tp % 3
+        return xp[(g + t) * WINDOWS + s + n, pl.ds(7 + p + par, HALF, stride=2), :]
+
+    per = 3 * HT
+    for s in range(WT // 2):
+        for g in range(3):
+            for par in range(2):
+                row = s * per + g * HT + par * HALF
+                for n in range(5):
+                    y = window(2 * n, g, s, par, 2)
+                    if n < 4:
+                        y = jnp.where(low, y, window(2 * n + 1, g, s, par, 0))
+                    at[row : row + HALF, n * 128 : (n + 1) * 128] = (y * mask[g][n]).astype(BF)
+        if s % GROUP == GROUP - 1:
+            rows = slice((s + 1 - GROUP) * per, (s + 1) * per)
+            v = jnp.dot(at[rows, :], wb[...], preferred_element_type=F32)
+            for k in range(GROUP * 6):
+                s2, g, par = s + 1 - GROUP + k // 6, k // 2 % 3, k % 2
+                ref = (even, odd)[par]
+                for q in range(6):
+                    j, c = q // 3, q % 3
+                    u = v[k * HALF : (k + 1) * HALF, q * 128 : (q + 1) * 128]
+                    u = u + 0.5 * bias(bin_ref, c)
+                    u = times(u * (1.0 + jnp.tanh(u)), m_mid[g]).astype(BF).astype(F32)
+                    ref[3 * g + c, pl.ds(TOP + 2 * s2 + j, HALF, stride=PITCH), :] = u
 
     for cp in by_col:
         cp.wait()
@@ -229,11 +246,10 @@
     for cp in both:
         cp.wait()
 
-    def emit(m, c):
+    def emit(m, c, plain, diff):
         at_row = lambda ref, k, off: ref[k, m * PITCH + off : m * PITCH + off + WT, :]
-        slot = m % 4
-
-        def columns(plain, diff, k):
+
+        def columns(k):
             x = at_row(plain, 3 * k + c, 0)
             return x - at_row(diff, 4 * c + 2 * k, 0), x + at_row(diff, 4 * c + 2 * k + 1, 1)
 
@@ -242,33 +258,45 @@
             base = x - at_row(r_sd, c, 0), x + at_row(r_sd, 3 + c, 1)
         else:
             base = bias(bmid_ref, c), bias(bmid_ref, c)
-        rows = {4 * m - 1: (r_ms, r_md, 1), 4 * m: (r_ms, r_md, 0)}
-        rows.update({4 * m + 1: (r_ps, r_pd, 1), 4 * m + 2: (r_ps, r_pd, 0)})
-        for n, (u, (plain, diff, k)) in enumerate(rows.items()):
-            if 0 <= u < 2 * HT and (m < HALF or n == 0):
-                y = columns(plain, diff, k)
+        pair = ((4 * m - 1, 1), (4 * m, 0)) if plain is r_ms else ((4 * m + 1, 1), (4 * m + 2, 0))
+        for u, k in pair:
+            if 0 <= u < 2 * HT:
+                y = columns(k)
+                n = u % 16
                 for b in range(2):
-                    st[c, slot, n, pl.ds(b, WT, stride=2), :] = base[b] + y[b]
-                ob[u, :, c * 128 : (c + 1) * 128] = st[c, slot, n].astype(BF)
-
-    def diff_part(c):
-        for out, lhs, w in ((r_md, lmd, w_m), (r_pd, lpd, w_p)):
-            weights = [w[k, :, c * 128 : (c + 1) * 128] for k in range(4)]
-            mm(out, 4 * c, lhs, jnp.concatenate(weights, axis=1))
-
-    def out_part(c):
+                    st[c, n, pl.ds(b, WT, stride=2), :] = base[b] + y[b]
+                ob[u, :, c * 128 : (c + 1) * 128] = st[c, n].astype(BF)
+
+    def diff_part(c, out, lhs, w):
+        weights = [w[k, :, c * 128 : (c + 1) * 128] for k in range(4)]
+        mm(out, 4 * c, lhs, jnp.concatenate(weights, axis=1))
+
+    m_part = lambda c: diff_part(c, r_md, lmd, w_m)
+    p_part = lambda c: diff_part(c, r_pd, lpd, w_p)
+
+    def m_out(c):
         for m in range(HALF + 1):
-            emit(m, c)
-            if c == 2 and m % 4 == 0 and m > 0:
-                block = pl.ds(4 * m - 16, 16)
+            emit(m, c, r_ms, r_md)
+
+    def p_out(c):
+        for m in range(HALF):
+            emit(m, c, r_ps, r_pd)
+            if c == 2 and m % 2 == 1:
+                block = pl.ds(4 * m - 4, 8)
                 pltpu.make_async_copy(ob.at[block], out_hbm.at[0, block], osem).start()
 
-    diff_part(0)
-    diff_part(1)
-    out_part(0)
-    diff_part(2)
-    out_part(1)
-    out_part(2)
+    m_part(0)
+    p_part(0)
+    m_part(1)
+    m_out(0)
+    p_part(1)
+    p_out(0)
+    m_part(2)
+    m_out(1)
+    p_part(2)
+    p_out(1)
+    m_out(2)
+    p_out(2)
     pltpu.make_async_copy(ob, out_hbm.at[0], osem).wait()
 
 
@@ -283,9 +311,9 @@
         out_shape=jax.ShapeDtypeStruct((1, 2 * HT, 2 * WT, CH), BF),
         scratch_shapes=[
             pltpu.VMEM((3, HT * 8, 128), F32),
-            pltpu.VMEM((5 * STRIP, HT + 16, 128), F32),
-            pltpu.VMEM((9, 128, CH), BF),
-            pltpu.VMEM((KIN, SW * CH), BF),
+            pltpu.VMEM((5 * WINDOWS, HT + 16, 128), F32),
+            pltpu.VMEM((KPAIR, 2 * CH), BF),
+            pltpu.VMEM((3 * HT * WT // 2, KPAIR), BF),
             pltpu.VMEM((9, TOP + MORE, 128), F32),
             pltpu.VMEM((9, TOP + MORE, 128), F32),
             pltpu.VMEM((FULL, KMID), BF),
@@ -303,7 +331,7 @@
             pltpu.VMEM((12, MORE, 128), F32),
             pltpu.VMEM((6, FULL, 128), F32),
             pltpu.VMEM((12, FULL, 128), F32),
-            pltpu.VMEM((3, 4, 4, 2 * WT, 128), F32),
+            pltpu.VMEM((3, 16, 2 * WT, 128), F32),
             pltpu.VMEM((2 * HT, 2 * WT, CH), BF),
             pltpu.SemaphoreType.DMA((18,)),
             pltpu.SemaphoreType.DMA,

time: 36.2 us -> 35.5 us (0.981)
  Pallas kernels: 19.5 us -> 18.8 us
    pallas_call x1, Pallas kernels: 12.3 us -> 11.7 us  [decode(): pl.pallas_call(main_body, in_specs=[smem, smem, vmem, vmem, vmem, vmem, v...]
where the time goes in v3:
time: 35.5 us; the launch traced here: 35.2 us
  Pallas kernels  18.8 us (53%)
  starting transfers between devices  13.5 us (38%)
  waiting for transfers between devices  2.05 us (6%)
  local copies, waits for them, and re-layouts  0.77 us (2%)
    pallas_call x1, Pallas kernels, decode(): pl.pallas_call(main_body, in_specs=[smem, smem, vmem, vmem, vmem, vmem, v...  11.7 us
    all_to_all x1, starting transfers between devices, on_device(): lax.all_to_all(patch(before, slots(latents)), 'tm', split_axis=0, concat_...  9.46 us
    pallas_call x1, Pallas kernels, prep(): pl.pallas_call(prep_body, in_specs=[hbm], out_specs=[vmem, vmem, hbm, hbm...  6.4 us
    ppermute x1, starting transfers between devices, on_device(): lax.ppermute(latents, 'req', [(i, i + 1) for i in range(groups - 1)])  4.01 us
    all_to_all x1, waiting for transfers between devices, on_device(): lax.all_to_all(patch(before, slots(latents)), 'tm', split_axis=0, concat_...  1.77 us
    unnamed x10, local copies, waits for them, and re-layouts  0.77 us
  transfers between devices with their start and end apart: 2, of which 2 were waited for; matrix products, arithmetic and copies ran while one was open for 0% of the time, Pallas kernels for 18%

profile of v3, /device:TPU:1, one launch (start us, length us, event | category | flops | bytes accessed | tf_op | source)
XLA Modules:
  0.0 35.2 jit_solution(7466082322638121607)
XLA Ops:
  0.0 4.0 %collective-permute-start = (bf16[32,384]{1,0:T(8,128)(2,1)}, bf16[32,384]{1,0:T(8,128)(2,1)S(1)}, u32[]{:S(2)}, u32[]{:S(2)}) collective-permute-start(bf16[32,384]{1,0:T(8,128)(2,1)} %own_ref.1), channel_id=1, source_target_pairs={{0,32},{32,64},{64,96},{1,33},{33,65},{65,97},{2,34},{34,66},{66,9... | collective-permute-start | bytes 73736 | tf_op jit(solution)/shard_map/ppermute | solution.py:346
  4.0 0.0 copy-start.1
  4.0 0.7 %copy-done.1 = bf16[32,384]{1,0:T(8,128)(2,1)S(1)} copy-done((bf16[32,384]{1,0:T(8,128)(2,1)S(1)}, bf16[32,384]{1,0:T(8,128)(2,1)}, u32[]{:S(2)}) %copy-start.1) | copy-done | bytes 24600
  4.8 0.1 slots.1.s_ref
  4.9 0.3 collective-permute-done.before_ref
  5.2 0.7 %patch.1 = bf16[32,8,384]{2,1,0:T(8,128)(2,1)} custom-call(bf16[32,384]{1,0:T(8,128)(2,1)S(1)} %collective-permute-done.before_ref, bf16[32,8,384]{2,1,0:T(8,128)(2,1)S(1)} %slots.1.s_ref), custom_call_target="tpu_custom_call" | custom-call | tf_op jit(solution)/shard_map/patch/pallas_call | solution.py:116
  5.9 9.5 %all-to-all-start = ((bf16[32,8,384]{2,1,0:T(8,128)(2,1)}), bf16[32,8,384]{2,1,0:T(8,128)(2,1)S(1)}, u32[]{:S(2)}, u32[]{:S(2)}) async-start(bf16[32,8,384]{2,1,0:T(8,128)(2,1)} %patch.1), calls=%async_computation | async-start | bytes 393216 | tf_op jit(solution)/shard_map/all_to_all | solution.py:347
  15.3 0.0 copy-start
  15.3 0.0 copy-start.2
  15.3 0.0 copy-start.3
  15.4 0.0 copy-start.4
  15.4 6.4 %prep.1 = (bf16[1152,384]{1,0:T(8,128)(2,1)S(1)}, bf16[1152,768]{1,0:T(8,128)(2,1)S(1)}, bf16[2,1152,768]{2,1,0:T(8,128)(2,1)}, bf16[4,1152,384]{2,1,0:T(8,128)(2,1)}) custom-call(bf16[3,3,3,384,384]{4,3,2,1,0:T(8,128)(2,1)} %w_hbm.3), custom_call_target="tpu_custom_call" | custom-call | tf_op jit(solution)/shard_map/prep/pallas_call | solution.py:64
  21.8 1.8 %all-to-all-done.x_ref = bf16[32,8,384]{2,1,0:T(8,128)(2,1)S(1)} async-done(((bf16[32,8,384]{2,1,0:T(8,128)(2,1)}), bf16[32,8,384]{2,1,0:T(8,128)(2,1)S(1)}, u32[]{:S(2)}, u32[]{:S(2)}) %all-to-all-start) | async-done | bytes 196640 | tf_op jit(solution)/shard_map/all_to_all | solution.py:347
  23.6 0.0 copy-done
  23.6 0.0 copy-done.2
  23.6 0.0 copy-done.3
  23.6 0.0 copy-done.4
  23.6 11.7 %decode.1 = bf16[1,64,48,384]{3,2,1,0:T(8,128)(2,1)} custom-call(s32[1]{0:T(128)} %bitcast.pos_ref, s32[8]{0:T(128)S(1)} %copy-done.4, bf16[32,8,384]{2,1,0:T(8,128)(2,1)S(1)} %all-to-all-done.x_ref, bf16[432,384]{1,0:T(8,128)(2,1)S(1)} %bitcast.2, f32[384]{0:T(512)S(1)} %copy-done.2, f32[384]{0:T(512)S(1)} %copy-done.3, ...), custom_call_target="tpu_custom_call" | custom-call | tf_op jit(solution)/shard_map/decode/pallas_call | solution.py:307
Async XLA Ops:
  0.0 5.2 %collective-permute-start = (bf16[32,384]{1,0:T(8,128)(2,1)}, bf16[32,384]{1,0:T(8,128)(2,1)S(1)}, u32[]{:S(2)}, u32[]{:S(2)}) collective-permute-start(bf16[32,384]{1,0:T(8,128)(2,1)} %own_ref.1), channel_id=1, source_target_pairs={{0,32},{32,64},{64,96},{1,33},{33,65},{65,97},{2,34},{34,66},{66,9... | collective-permute-start | bytes 73736 | tf_op jit(solution)/shard_map/ppermute | solution.py:346
  4.0 0.8 %copy-start.1 = (bf16[32,384]{1,0:T(8,128)(2,1)S(1)}, bf16[32,384]{1,0:T(8,128)(2,1)}, u32[]{:S(2)}) copy-start(bf16[32,384]{1,0:T(8,128)(2,1)} %own_ref.1) | copy-start | bytes 73732
  5.9 17.7 %all-to-all-start = ((bf16[32,8,384]{2,1,0:T(8,128)(2,1)}), bf16[32,8,384]{2,1,0:T(8,128)(2,1)S(1)}, u32[]{:S(2)}, u32[]{:S(2)}) async-start(bf16[32,8,384]{2,1,0:T(8,128)(2,1)} %patch.1), calls=%async_computation | async-start | bytes 393216 | tf_op jit(solution)/shard_map/all_to_all | solution.py:347
  15.3 8.2 %copy-start = (bf16[3,3,3,16,384]{4,3,2,1,0:T(8,128)(2,1)S(1)}, bf16[3,3,3,16,384]{4,3,2,1,0:T(8,128)(2,1)}, u32[]{:S(2)}) copy-start(bf16[3,3,3,16,384]{4,3,2,1,0:T(8,128)(2,1)} %param.8) | copy-start | bytes 995332
  15.3 8.2 %copy-start.2 = (f32[384]{0:T(512)S(1)}, f32[384]{0:T(512)}, u32[]{:S(2)}) copy-start(f32[384]{0:T(512)} %bin_ref.1) | copy-start | bytes 4612
  15.3 8.2 %copy-start.3 = (f32[384]{0:T(512)S(1)}, f32[384]{0:T(512)}, u32[]{:S(2)}) copy-start(f32[384]{0:T(512)} %bmid_ref.1) | copy-start | bytes 4612
  15.4 8.2 %copy-start.4 = (s32[8]{0:T(128)S(1)}, s32[8]{0:T(128)}, u32[]{:S(2)}) copy-start(s32[8]{0:T(128)} %len_ref.1) | copy-start | bytes 100
